TPU v7x, 512 devices: a whole 4x4x16 slice. The times are simulated.
512 devices in a mesh: ctx: 512 (over x, z, y, core).
Axes of the slice: x: 4, y: 4, z: 16, core: 2. Of those that a mesh axis runs over, the one named last changes fastest.
Arguments:
- queries: bfloat16 [65536, 16, 128], P('ctx'), may hold values from -6 to 6
- keys: bfloat16 [65536, 8, 128], P('ctx'), may hold values from -5 to 5
- values: bfloat16 [65536, 8, 128], P('ctx'), may hold values from -6 to 6
- d_out: bfloat16 [65536, 16, 128], P('ctx'), may hold values from -48 to 48
Outputs:
- grad_queries: bfloat16 [65536, 16, 128], P('ctx')
- grad_keys: bfloat16 [65536, 8, 128], P('ctx')
- grad_values: bfloat16 [65536, 8, 128], P('ctx')
All inputs are finite; a program needn't handle non-finite values.
Results may differ from a plain program's by a relative error of at most 0.012.
The roundings to bfloat16 on the way count: a program that leaves them out, or rounds other values in their place, can miss the bound.
Values may be sent and summed in bfloat16 or wider, within the bound.
A program may use at most 64 MiB of HBM per device.

v0:
```python
import jax
import jax.numpy as jnp
from jax import lax
from jax.sharding import PartitionSpec as P

HEADS = 16
KV_HEADS = 8
HEAD_WIDTH = 128
WINDOW = 512
TOK_DEV = 128


score_scale = 168.0 ** (-0.5)


def from_behind(shard, axis, by):
    peers = lax.axis_size(axis)
    pairs = [(i, i + by) for i in range(peers) if 0 <= i + by < peers]
    return lax.ppermute(shard, axis, pairs)


def window_grads(queries, keys_win, values_win, d_out, row_start):
    row_count = queries.shape[0]
    key_span = keys_win.shape[0]
    group_size = HEADS // KV_HEADS
    grouped = queries.reshape(row_count, KV_HEADS, group_size, HEAD_WIDTH)
    gradient_per_group = d_out.reshape(row_count, KV_HEADS, group_size, HEAD_WIDTH)
    scores = (
        jnp.einsum("tgre,jge->grtj", grouped, keys_win, preferred_element_type=jnp.float32)
        * score_scale
    )
    query_pos = row_start + jnp.arange(row_count, dtype=jnp.int32)
    key_pos = row_start - WINDOW + jnp.arange(key_span, dtype=jnp.int32)
    distance = query_pos[:, None] - key_pos[None, :]
    visible = (distance >= 0) & (distance < WINDOW) & (key_pos[None, :] >= 0)
    scores = jnp.where(visible, scores, -jnp.inf)
    row_max = jnp.max(scores, axis=-1, keepdims=True)
    row_sum = jnp.sum(jnp.exp(scores - row_max), axis=-1, keepdims=True)
    log_total = row_max + jnp.log(row_sum)
    probability = jnp.exp(scores - log_total)
    probs_low = probability.astype(jnp.bfloat16)
    attention_result_rows = jnp.einsum(
        "grtj,jge->tgre", probs_low, values_win, preferred_element_type=jnp.float32
    ).astype(jnp.bfloat16)
    row_dot_product = jnp.einsum(
        "cqzj,cqzj->qzc",
        gradient_per_group,
        attention_result_rows,
        preferred_element_type=jnp.float32,
    )
    grad_probs = jnp.einsum(
        "tgre,jge->grtj", gradient_per_group, values_win, preferred_element_type=jnp.float32
    )
    grad_scores = (probability * (grad_probs - row_dot_product[..., None])).astype(jnp.bfloat16)
    query_gradient = (
        jnp.einsum("grtj,jge->tgre", grad_scores, keys_win, preferred_element_type=jnp.float32)
        * score_scale
    )
    grad_key = (
        jnp.einsum("grtj,tgre->jge", grad_scores, grouped, preferred_element_type=jnp.float32)
        * score_scale
    )
    grad_value = jnp.einsum(
        "grtj,tgre->jge", probs_low, gradient_per_group, preferred_element_type=jnp.float32
    )
    query_gradient = query_gradient.astype(jnp.bfloat16).reshape(row_count, HEADS, HEAD_WIDTH)
    return (query_gradient, grad_key, grad_value)


def body(queries, keys, values, d_out):
    halo_depth = WINDOW // TOK_DEV
    row_count = queries.shape[0]
    own_pair = jnp.stack([keys, values])
    preceding_shard = [from_behind(own_pair, "ctx", offset) for offset in range(halo_depth, 0, -1)]
    window_pair = jnp.concatenate(preceding_shard + [own_pair], axis=1)
    row_start = lax.axis_index("ctx") * row_count
    query_gradient, grad_key, grad_value = window_grads(
        queries, window_pair[0], window_pair[1], d_out, row_start
    )
    partials = jnp.stack([grad_key, grad_value]).reshape(
        2, halo_depth + 1, row_count, KV_HEADS, HEAD_WIDTH
    )
    summed = partials[:, halo_depth]
    for offset in range(1, halo_depth + 1):
        summed = summed + from_behind(
            partials[:, halo_depth - offset].astype(jnp.bfloat16), "ctx", -offset
        ).astype(jnp.float32)
    return (query_gradient, summed[0].astype(jnp.bfloat16), summed[1].astype(jnp.bfloat16))


def solution(mesh):
    placed = (
        P("ctx", None, None),
        P("ctx", None, None),
        P("ctx", None, None),
        P("ctx", None, None),
    )
    return jax.shard_map(
        body,
        mesh=mesh,
        in_specs=placed,
        out_specs=(P("ctx", None, None), P("ctx", None, None), P("ctx", None, None)),
        check_vma=False,
    )
```

profile of v0, /device:TPU:6, one launch (start us, length us, event | category | flops | bytes accessed | tf_op | source)
XLA Modules:
  0.0 141.9 jit_solution(8701596121673252261)
XLA Ops:
  0.6 1.2 copy_bitcast_fusion.1
  1.9 1.9 %collective-permute-start.3 = (bf16[2,128,8,128]{3,1,2,0:T(8,128)(2,1)S(1)}, bf16[2,128,8,128]{3,1,2,0:T(8,128)(2,1)S(1)}, u32[]{:S(2)}, u32[]{:S(2)}) collective-permute-start(bf16[2,128,8,128]{3,1,2,0:T(8,128)(2,1)S(1)} %pad_maximum_fusion), channel_id=1, source_target_pairs={{0,1},{1,2},{2,3},{3,4},{4,5},{5,6},{6,7},{7,8},{8,9},{9,10},{10,1... | collective-permute-start | bytes 1572872 | tf_op jit(solution)/shard_map/ppermute | solution.py:19
  3.8 3.5 %collective-permute-start.2 = (bf16[2,128,8,128]{3,1,2,0:T(8,128)(2,1)S(1)}, bf16[2,128,8,128]{3,1,2,0:T(8,128)(2,1)S(1)}, u32[]{:S(2)}, u32[]{:S(2)}) collective-permute-start(bf16[2,128,8,128]{3,1,2,0:T(8,128)(2,1)S(1)} %pad_maximum_fusion), channel_id=1, source_target_pairs={{0,2},{1,3},{2,4},{3,5},{4,6},{5,7},{6,8},{7,9},{8,10},{9,11},{10,... | collective-permute-start | bytes 1572872 | tf_op jit(solution)/shard_map/ppermute | solution.py:19
  7.3 4.2 %collective-permute-start.1 = (bf16[2,128,8,128]{3,1,2,0:T(8,128)(2,1)S(1)}, bf16[2,128,8,128]{3,1,2,0:T(8,128)(2,1)S(1)}, u32[]{:S(2)}, u32[]{:S(2)}) collective-permute-start(bf16[2,128,8,128]{3,1,2,0:T(8,128)(2,1)S(1)} %pad_maximum_fusion), channel_id=1, source_target_pairs={{0,3},{1,4},{2,5},{3,6},{4,7},{5,8},{6,9},{7,10},{8,11},{9,12},{10... | collective-permute-start | bytes 1572872 | tf_op jit(solution)/shard_map/ppermute | solution.py:19
  11.5 5.1 %collective-permute-start = (bf16[2,128,8,128]{3,1,2,0:T(8,128)(2,1)S(1)}, bf16[2,128,8,128]{3,1,2,0:T(8,128)(2,1)}, u32[]{:S(2)}, u32[]{:S(2)}) collective-permute-start(bf16[2,128,8,128]{3,1,2,0:T(8,128)(2,1)S(1)} %pad_maximum_fusion), channel_id=1, source_target_pairs={{0,4},{1,5},{2,6},{3,7},{4,8},{5,9},{6,10},{7,11},{8,12},{9,13},{1... | collective-permute-start | bytes 1572872 | tf_op jit(solution)/shard_map/ppermute | solution.py:19
  16.9 31.7 %collective-permute-done = bf16[2,128,8,128]{3,1,2,0:T(8,128)(2,1)} collective-permute-done((bf16[2,128,8,128]{3,1,2,0:T(8,128)(2,1)S(1)}, bf16[2,128,8,128]{3,1,2,0:T(8,128)(2,1)}, u32[]{:S(2)}, u32[]{:S(2)}) %collective-permute-start) | collective-permute-done | bytes 524320 | tf_op jit(solution)/shard_map/ppermute | solution.py:19
  52.1 1.2 copy-done.2
  53.3 1.4 %convolution_convert_fusion = bf16[8,128,2,128]{3,1,2,0:T(8,128)(2,1)S(1)} fusion(bf16[2,640,8,128]{3,1,2,0:T(8,128)(2,1)S(1)} %constant_dynamic-update-slice_fusion, f32[8,640,128,2]{2,1,3,0:T(8,128)S(1)} %get-tuple-element.13, f32[8,2,128]{2,1,0:T(2,128)S(1)} %bitcast.108, pred[128,640]{0,1:T(8,128)(4,1)S(1)} %fusion.18), kind=kOutput, calls=%fused_computation.15 | convolution fusion | flops 341049344 | bytes 7168000 | tf_op jit(solution)/shard_map/grtj,jge->tgre/dot_general | solution.py:42
  55.3 1.6 %copy.26 = f32[8,2,128,128]{3,1,0,2:T(2,128)S(1)} copy(f32[8,2,128,128]{2,1,3,0:T(2,128)S(1)} %fusion.11) | data formatting | bytes 2097152
  58.3 3.9 %fusion.12 = f32[8,640,128,1]{2,1,3,0:T(8,128)S(1)} fusion(bf16[128,8,2,128]{3,2,1,0:T(2,128)(2,1)S(1)} %bitcast.104, f32[8,640,128,2]{2,1,3,0:T(8,128)} %copy-done.2, f32[8,2,128]{2,1,0:T(2,128)S(1)} %bitcast.109, pred[128,640]{0,1:T(8,128)(4,1)S(1)} %fusion.18), kind=kOutput, calls=%fused_computation.33 | convolution fusion | flops 340787200 | bytes 8478720 | tf_op jit(solution)/shard_map/grtj,tgre->jge/dot_general | solution.py:63
  63.0 1.7 %fusion.1 = bf16[8,2,128,640]{2,3,1,0:T(8,128)(2,1)S(1)} fusion(f32[8,640,128,2]{2,1,3,0:T(8,128)S(1)} %bitcast.100, f32[8,2,128]{2,1,0:T(2,128)S(1)} %copy.27, f32[8,2,128]{2,1,0:T(2,128)S(1)} %bitcast.110, pred[128,640]{0,1:T(8,128)(4,1)S(1)} %fusion.18, bf16[2,640,8,128]{3,1,2,0:T(8,128)(2,1)S(1)} %copy-done.4, bf16[128,8,2,128]{3,2,1,0:T(2,128)(2,1)S(1)} %bitcast.105), kind=kOutput, calls=%fused_computation.2 | convolution fusion | flops 343408640 | bytes 9797632 | tf_op jit(solution)/shard_map/tgre,jge->grtj/dot_general | solution.py:51
  65.6 1.5 %copy_dynamic-update-slice_fusion.1 = f32[2,5,128,8,128]{4,3,2,0,1:T(8,128)S(1)} fusion(f32[1,5,128,8,128]{4,2,1,3,0:T(8,128)S(1)} %bitcast.98), kind=kLoop, calls=%fused_computation.10 | loop fusion | bytes 5242880
  67.1 1.5 %copy_dynamic-update-slice_fusion = f32[2,5,128,8,128]{4,3,2,0,1:T(8,128)S(1)} fusion(f32[2,5,128,8,128]{4,3,2,0,1:T(8,128)S(1)} %copy_dynamic-update-slice_fusion.1, f32[1,5,128,8,128]{4,2,1,3,0:T(8,128)S(1)} %bitcast.101), kind=kLoop, calls=%fused_computation.9 | loop fusion | bytes 5242880 | tf_op jit(solution)/shard_map/stack | solution.py:80
  69.1 1.8 %copy-done.1 = f32[2,5,128,8,128]{4,3,2,0,1:T(8,128)} copy-done((f32[2,5,128,8,128]{4,3,2,0,1:T(8,128)}, f32[2,5,128,8,128]{4,3,2,0,1:T(8,128)S(1)}, u32[]{:S(2)}) %copy-start.1) | copy-done | bytes 5242904
  70.9 1.4 slice_bitcast_fusion.10
  72.3 23.5 %collective-permute-start.4 = (bf16[2,128,8,128]{3,2,1,0:T(8,128)(2,1)}, bf16[2,128,8,128]{3,2,1,0:T(8,128)(2,1)S(1)}, u32[]{:S(2)}, u32[]{:S(2)}) collective-permute-start(bf16[2,128,8,128]{3,2,1,0:T(8,128)(2,1)} %get-tuple-element.6), channel_id=1, source_target_pairs={{1,0},{2,1},{3,2},{4,3},{5,4},{6,5},{7,6},{8,7},{9,8},{10,9},{11,1... | collective-permute-start | bytes 1572872 | tf_op jit(solution)/shard_map/ppermute | solution.py:19
  95.8 7.8 %collective-permute-start.7 = (bf16[2,128,8,128]{3,2,1,0:T(8,128)(2,1)}, bf16[2,128,8,128]{3,2,1,0:T(8,128)(2,1)S(1)}, u32[]{:S(2)}, u32[]{:S(2)}) collective-permute-start(bf16[2,128,8,128]{3,2,1,0:T(8,128)(2,1)} %get-tuple-element.7), channel_id=1, source_target_pairs={{4,0},{5,1},{6,2},{7,3},{8,4},{9,5},{10,6},{11,7},{12,8},{13,9},{1... | collective-permute-start | bytes 1572872 | tf_op jit(solution)/shard_map/ppermute | solution.py:19
  103.6 1.9 %collective-permute-start.6 = (bf16[2,128,8,128]{3,2,1,0:T(8,128)(2,1)}, bf16[2,128,8,128]{3,2,1,0:T(8,128)(2,1)S(1)}, u32[]{:S(2)}, u32[]{:S(2)}) collective-permute-start(bf16[2,128,8,128]{3,2,1,0:T(8,128)(2,1)} %get-tuple-element.8), channel_id=1, source_target_pairs={{3,0},{4,1},{5,2},{6,3},{7,4},{8,5},{9,6},{10,7},{11,8},{12,9},{13... | collective-permute-start | bytes 1572872 | tf_op jit(solution)/shard_map/ppermute | solution.py:19
  105.5 2.5 %collective-permute-start.5 = (bf16[2,128,8,128]{3,2,1,0:T(8,128)(2,1)}, bf16[2,128,8,128]{3,2,1,0:T(8,128)(2,1)S(1)}, u32[]{:S(2)}, u32[]{:S(2)}) collective-permute-start(bf16[2,128,8,128]{3,2,1,0:T(8,128)(2,1)} %get-tuple-element.9), channel_id=1, source_target_pairs={{2,0},{3,1},{4,2},{5,3},{6,4},{7,5},{8,6},{9,7},{10,8},{11,9},{12,... | collective-permute-start | bytes 1572872 | tf_op jit(solution)/shard_map/ppermute | solution.py:19
  108.7 1.2 copy.17
  109.9 11.2 %collective-permute-done.7 = bf16[2,128,8,128]{3,2,1,0:T(8,128)(2,1)S(1)} collective-permute-done((bf16[2,128,8,128]{3,2,1,0:T(8,128)(2,1)}, bf16[2,128,8,128]{3,2,1,0:T(8,128)(2,1)S(1)}, u32[]{:S(2)}, u32[]{:S(2)}) %collective-permute-start.7) | collective-permute-done | bytes 524320 | tf_op jit(solution)/shard_map/ppermute | solution.py:19
  121.1 12.8 %collective-permute-done.6 = bf16[2,128,8,128]{3,2,1,0:T(8,128)(2,1)S(1)} collective-permute-done((bf16[2,128,8,128]{3,2,1,0:T(8,128)(2,1)}, bf16[2,128,8,128]{3,2,1,0:T(8,128)(2,1)S(1)}, u32[]{:S(2)}, u32[]{:S(2)}) %collective-permute-start.6) | collective-permute-done | bytes 524320 | tf_op jit(solution)/shard_map/ppermute | solution.py:19
  133.9 5.6 %collective-permute-done.5 = bf16[2,128,8,128]{3,2,1,0:T(8,128)(2,1)S(1)} collective-permute-done((bf16[2,128,8,128]{3,2,1,0:T(8,128)(2,1)}, bf16[2,128,8,128]{3,2,1,0:T(8,128)(2,1)S(1)}, u32[]{:S(2)}, u32[]{:S(2)}) %collective-permute-start.5) | collective-permute-done | bytes 524320 | tf_op jit(solution)/shard_map/ppermute | solution.py:19
  139.5 1.5 %fusion.10 = bf16[2,128,8,128]{3,2,1,0:T(8,128)(2,1)S(1)} fusion(f32[2,5,128,8,128]{4,3,2,0,1:T(8,128)} %copy-done.1, bf16[2,128,8,128]{3,2,1,0:T(8,128)(2,1)S(1)} %collective-permute-done.7, bf16[2,128,8,128]{3,2,1,0:T(8,128)(2,1)S(1)} %collective-permute-done.6, bf16[2,128,8,128]{3,2,1,0:T(8,128)(2,1)S(1)} %collective-permute-done.5, ...), kind=kLoop, calls=%fused_computation.22 | loop fusion | flops 2359296 | bytes 3670016 | tf_op jit(solution)/shard_map/convert.1
  (39 shorter events, 9.2 us)
Async XLA Ops:
  0.6 49.5 %copy-start = (bf16[128,16,128]{2,1,0:T(8,128)(2,1)S(1)}, bf16[128,16,128]{2,1,0:T(8,128)(2,1)}, u32[]{:S(2)}) copy-start(bf16[128,16,128]{2,1,0:T(8,128)(2,1)} %param.4) | copy-start | bytes 1572868
  1.9 48.0 %collective-permute-start.3 = (bf16[2,128,8,128]{3,1,2,0:T(8,128)(2,1)S(1)}, bf16[2,128,8,128]{3,1,2,0:T(8,128)(2,1)S(1)}, u32[]{:S(2)}, u32[]{:S(2)}) collective-permute-start(bf16[2,128,8,128]{3,1,2,0:T(8,128)(2,1)S(1)} %pad_maximum_fusion), channel_id=1, source_target_pairs={{0,1},{1,2},{2,3},{3,4},{4,5},{5,6},{6,7},{7,8},{8,9},{9,10},{10,1... | collective-permute-start | bytes 1572872 | tf_op jit(solution)/shard_map/ppermute | solution.py:19
  3.8 46.0 %collective-permute-start.2 = (bf16[2,128,8,128]{3,1,2,0:T(8,128)(2,1)S(1)}, bf16[2,128,8,128]{3,1,2,0:T(8,128)(2,1)S(1)}, u32[]{:S(2)}, u32[]{:S(2)}) collective-permute-start(bf16[2,128,8,128]{3,1,2,0:T(8,128)(2,1)S(1)} %pad_maximum_fusion), channel_id=1, source_target_pairs={{0,2},{1,3},{2,4},{3,5},{4,6},{5,7},{6,8},{7,9},{8,10},{9,11},{10,... | collective-permute-start | bytes 1572872 | tf_op jit(solution)/shard_map/ppermute | solution.py:19
  7.3 42.4 %collective-permute-start.1 = (bf16[2,128,8,128]{3,1,2,0:T(8,128)(2,1)S(1)}, bf16[2,128,8,128]{3,1,2,0:T(8,128)(2,1)S(1)}, u32[]{:S(2)}, u32[]{:S(2)}) collective-permute-start(bf16[2,128,8,128]{3,1,2,0:T(8,128)(2,1)S(1)} %pad_maximum_fusion), channel_id=1, source_target_pairs={{0,3},{1,4},{2,5},{3,6},{4,7},{5,8},{6,9},{7,10},{8,11},{9,12},{10... | collective-permute-start | bytes 1572872 | tf_op jit(solution)/shard_map/ppermute | solution.py:19
  11.5 37.1 %collective-permute-start = (bf16[2,128,8,128]{3,1,2,0:T(8,128)(2,1)S(1)}, bf16[2,128,8,128]{3,1,2,0:T(8,128)(2,1)}, u32[]{:S(2)}, u32[]{:S(2)}) collective-permute-start(bf16[2,128,8,128]{3,1,2,0:T(8,128)(2,1)S(1)} %pad_maximum_fusion), channel_id=1, source_target_pairs={{0,4},{1,5},{2,6},{3,7},{4,8},{5,9},{6,10},{7,11},{8,12},{9,13},{1... | collective-permute-start | bytes 1572872 | tf_op jit(solution)/shard_map/ppermute | solution.py:19
  50.1 2.0 %copy-start.3 = (bf16[2,640,8,128]{3,1,2,0:T(8,128)(2,1)}, bf16[2,640,8,128]{3,1,2,0:T(8,128)(2,1)S(1)}, u32[]{:S(2)}) copy-start(bf16[2,640,8,128]{3,1,2,0:T(8,128)(2,1)S(1)} %constant_dynamic-update-slice_fusion) | copy-start | bytes 7864324
  51.0 2.3 %copy-start.2 = (f32[8,640,128,2]{2,1,3,0:T(8,128)}, f32[8,640,128,2]{2,1,3,0:T(8,128)S(1)}, u32[]{:S(2)}) copy-start(f32[8,640,128,2]{2,1,3,0:T(8,128)S(1)} %get-tuple-element.13) | copy-start | bytes 15728644
  54.7 2.2 %copy-start.5 = (bf16[128,16,128]{2,1,0:T(8,128)(2,1)S(1)}, bf16[128,16,128]{2,1,0:T(8,128)(2,1)}, u32[]{:S(2)}) copy-start(bf16[128,16,128]{2,1,0:T(8,128)(2,1)} %param.7) | copy-start | bytes 1572868
  58.1 4.1 %slice-start = ((s8[5242880]{0:T(1024)(128)(4,1)}), s8[1048576]{0:T(1024)(128)(4,1)S(1)}, s32[]{:S(2)}) async-start(s8[5242880]{0:T(1024)(128)(4,1)} %bitcast.99), calls=%async_computation | async-start | bytes 2097152
  58.3 3.9 %slice-start.1 = ((s8[5242880]{0:T(1024)(128)(4,1)}), s8[4194304]{0:T(1024)(128)(4,1)S(1)}, s32[]{:S(2)}) async-start(s8[5242880]{0:T(1024)(128)(4,1)} %bitcast.99), calls=%async_computation.1 | async-start | bytes 8388608
  58.3 4.7 %copy-start.4 = (bf16[2,640,8,128]{3,1,2,0:T(8,128)(2,1)S(1)}, bf16[2,640,8,128]{3,1,2,0:T(8,128)(2,1)}, u32[]{:S(2)}) copy-start(bf16[2,640,8,128]{3,1,2,0:T(8,128)(2,1)} %copy-done.3) | copy-start | bytes 7864324
  68.6 2.3 %copy-start.1 = (f32[2,5,128,8,128]{4,3,2,0,1:T(8,128)}, f32[2,5,128,8,128]{4,3,2,0,1:T(8,128)S(1)}, u32[]{:S(2)}) copy-start(f32[2,5,128,8,128]{4,3,2,0,1:T(8,128)S(1)} %copy_dynamic-update-slice_fusion) | copy-start | bytes 15728644
  72.3 37.6 %collective-permute-start.4 = (bf16[2,128,8,128]{3,2,1,0:T(8,128)(2,1)}, bf16[2,128,8,128]{3,2,1,0:T(8,128)(2,1)S(1)}, u32[]{:S(2)}, u32[]{:S(2)}) collective-permute-start(bf16[2,128,8,128]{3,2,1,0:T(8,128)(2,1)} %get-tuple-element.6), channel_id=1, source_target_pairs={{1,0},{2,1},{3,2},{4,3},{5,4},{6,5},{7,6},{8,7},{9,8},{10,9},{11,1... | collective-permute-start | bytes 1572872 | tf_op jit(solution)/shard_map/ppermute | solution.py:19
  95.8 25.3 %collective-permute-start.7 = (bf16[2,128,8,128]{3,2,1,0:T(8,128)(2,1)}, bf16[2,128,8,128]{3,2,1,0:T(8,128)(2,1)S(1)}, u32[]{:S(2)}, u32[]{:S(2)}) collective-permute-start(bf16[2,128,8,128]{3,2,1,0:T(8,128)(2,1)} %get-tuple-element.7), channel_id=1, source_target_pairs={{4,0},{5,1},{6,2},{7,3},{8,4},{9,5},{10,6},{11,7},{12,8},{13,9},{1... | collective-permute-start | bytes 1572872 | tf_op jit(solution)/shard_map/ppermute | solution.py:19
  103.6 30.3 %collective-permute-start.6 = (bf16[2,128,8,128]{3,2,1,0:T(8,128)(2,1)}, bf16[2,128,8,128]{3,2,1,0:T(8,128)(2,1)S(1)}, u32[]{:S(2)}, u32[]{:S(2)}) collective-permute-start(bf16[2,128,8,128]{3,2,1,0:T(8,128)(2,1)} %get-tuple-element.8), channel_id=1, source_target_pairs={{3,0},{4,1},{5,2},{6,3},{7,4},{8,5},{9,6},{10,7},{11,8},{12,9},{13... | collective-permute-start | bytes 1572872 | tf_op jit(solution)/shard_map/ppermute | solution.py:19
  105.5 34.0 %collective-permute-start.5 = (bf16[2,128,8,128]{3,2,1,0:T(8,128)(2,1)}, bf16[2,128,8,128]{3,2,1,0:T(8,128)(2,1)S(1)}, u32[]{:S(2)}, u32[]{:S(2)}) collective-permute-start(bf16[2,128,8,128]{3,2,1,0:T(8,128)(2,1)} %get-tuple-element.9), channel_id=1, source_target_pairs={{2,0},{3,1},{4,2},{5,3},{6,4},{7,5},{8,6},{9,7},{10,8},{11,9},{12,... | collective-permute-start | bytes 1572872 | tf_op jit(solution)/shard_map/ppermute | solution.py:19
where the time goes:
time: 142 us
  waiting for transfers between devices  61.4 us (43%)
  starting transfers between devices  50.4 us (35%)
  local copies, waits for them, and re-layouts  14.5 us (10%)
  matrix products  9.44 us (7%)
  other arithmetic  5.16 us (4%)
    ppermute x8, waiting for transfers between devices, from_behind(): return lax.ppermute(shard, axis, pairs)  61.4 us
    ppermute x8, starting transfers between devices, from_behind(): return lax.ppermute(shard, axis, pairs)  50.4 us
    unnamed x23, local copies, waits for them, and re-layouts  9.41 us
    dot_general x1, matrix products, window_grads(): jnp.einsum('grtj,tgre->jge', probs_low, gradient_per_group, preferred_ele...  3.89 us
  transfers between devices with their start and end apart: 8, of which 4 were waited for; matrix products, arithmetic and copies ran while one was open for 2% of the time, Pallas kernels for 0%

commit v1 on v0

v1 whole, which is shorter than its diff:
```python
import functools

import jax
import jax.numpy as jnp
from jax import lax
from jax.experimental import pallas as pl
from jax.experimental.pallas import tpu as pltpu
from jax.sharding import PartitionSpec as P

HEADS = 16
KV_HEADS = 8
HEAD_WIDTH = 128
WINDOW = 512
TOK_DEV = 128
GROUP = HEADS // KV_HEADS
CHIP_TOK = 2 * TOK_DEV
SPAN = WINDOW + CHIP_TOK
REACH = WINDOW + TOK_DEV
ROWS = GROUP * TOK_DEV
MINE = KV_HEADS // 2

MESH = pl.DeviceIdType.MESH
SCALE = 168.0 ** (-0.5)
F32 = jnp.float32
BF16 = jnp.bfloat16


def dot(a, b, contract):
    return lax.dot_general(a, b, ((contract[:1], contract[1:]), ((), ())), preferred_element_type=F32)


def kernel(
    n, kv_in, qd_in, dq_out, dkv_out,
    kvb, qdb, acc, p0_out, p0_in, s_out, s_in, dq_send, dkv_send,
    loc_kv, loc_qd, xkv_s, xkv_r, xqd_s, xqd_r, own_s, own_r, fwd_s, fwd_r,
    p0_s, p0_r, sum_s, sum_r, dq_s, dq_r, dkv_s, dkv_r,
):
    me = lax.axis_index("ctx")
    chip = me // 2
    core = me % 2
    other = 1 - core
    partner = chip * 2 + other
    ahead = (me + 2) % n
    ahead_other = (partner + 2) % n
    behind = (me + n - 2) % n
    behind_other = (partner + n - 2) % n

    barrier = pltpu.get_barrier_semaphore()
    for peer in (partner, ahead, ahead_other, behind, behind_other):
        pl.semaphore_signal(barrier, inc=1, device_id=(peer,), device_id_type=MESH)
    pl.semaphore_wait(barrier, 5)

    def remote(src, dst, send, recv, target):
        return pltpu.make_async_remote_copy(
            src_ref=src, dst_ref=dst, send_sem=send, recv_sem=recv, device_id=(target,), device_id_type=MESH
        )

    my_tok = pl.ds(pl.multiple_of(core * TOK_DEV, TOK_DEV), TOK_DEV)
    my_key = pl.ds(pl.multiple_of(WINDOW + core * TOK_DEV, TOK_DEV), TOK_DEV)
    my_back = pl.ds(pl.multiple_of(CHIP_TOK + core * TOK_DEV, TOK_DEV), TOK_DEV)
    my_row = pl.ds(pl.multiple_of(core * ROWS, ROWS), ROWS)
    other_tok = pl.ds(pl.multiple_of(WINDOW + other * TOK_DEV, TOK_DEV), TOK_DEV)
    other_row = pl.ds(pl.multiple_of(other * ROWS, ROWS), ROWS)

    def local_kv(h):
        return pltpu.make_async_copy(kv_in.at[core * MINE + h], kvb.at[h, :, my_key, :], loc_kv.at[h])

    def local_qd(h):
        return pltpu.make_async_copy(qd_in.at[core * MINE + h], qdb.at[h, :, my_row, :], loc_qd.at[h])

    def swap_kv(h):
        return remote(kv_in.at[other * MINE + h], kvb.at[h, :, my_key, :], xkv_s.at[h], xkv_r.at[h], partner)

    def swap_qd(h):
        return remote(qd_in.at[other * MINE + h], qdb.at[h, :, my_row, :], xqd_s.at[h], xqd_r.at[h], partner)

    def own_same(h):
        return remote(kv_in.at[core * MINE + h], kvb.at[h, :, my_back, :], own_s.at[h, 0], own_r.at[h, core], ahead)

    def own_cross(h):
        return remote(kv_in.at[other * MINE + h], kvb.at[h, :, my_back, :], own_s.at[h, 1], own_r.at[h, core], ahead_other)

    def came(h, j):
        tok = pl.ds(CHIP_TOK + j * TOK_DEV, TOK_DEV)
        return remote(kvb.at[h, :, tok, :], kvb.at[h, :, tok, :], own_s.at[h, j], own_r.at[h, j], ahead)

    def relay(h):
        return remote(
            kvb.at[h, :, pl.ds(CHIP_TOK, CHIP_TOK), :], kvb.at[h, :, pl.ds(0, CHIP_TOK), :], fwd_s.at[h], fwd_r.at[h], ahead
        )

    def far(h):
        return remote(p0_out.at[h], p0_in.at[h], p0_s.at[h], p0_r.at[h], behind)

    def near(h):
        return remote(s_out.at[h], s_in.at[h], sum_s.at[h], sum_r.at[h], behind)

    def give_dq(h):
        return remote(dq_send.at[h], dq_out.at[core * MINE + h], dq_s.at[h], dq_r.at[h], partner)

    def take_dq(h):
        return remote(dq_send.at[h], dq_out.at[other * MINE + h], dq_s.at[h], dq_r.at[h], partner)

    def give_dkv(h):
        return remote(dkv_send.at[h], dkv_out.at[core * MINE + h], dkv_s.at[h], dkv_r.at[h], partner)

    def take_dkv(h):
        return remote(dkv_send.at[h], dkv_out.at[other * MINE + h], dkv_s.at[h], dkv_r.at[h], partner)

    def send_own(h):
        own_same(h).start()
        own_cross(h).start()

    def pass_on(h):
        came(h, 0).wait_recv()
        came(h, 1).wait_recv()
        relay(h).start()

    send_own(0)
    for h in range(MINE):
        local_kv(h).start()
        local_qd(h).start()
        swap_kv(h).start()
        swap_qd(h).start()
        if h == 0:
            send_own(1)
    pass_on(0)
    send_own(2)

    first_key = WINDOW - CHIP_TOK * chip

    def half(h, b):
        key_at = pl.ds(b * TOK_DEV, REACH)
        row_at = pl.ds(b * ROWS, ROWS)
        k = kvb[h, 0, key_at, :]
        v = kvb[h, 1, key_at, :]
        q = qdb[h, 0, row_at, :]
        do = qdb[h, 1, row_at, :]
        s = dot(k, q, (1, 1))
        key_pos = lax.broadcasted_iota(jnp.int32, (REACH, ROWS), 0)
        query_pos = lax.broadcasted_iota(jnp.int32, (REACH, ROWS), 1) // GROUP
        distance = key_pos - query_pos
        visible = (distance > 0) & (distance <= WINDOW) & (key_pos >= first_key - b * TOK_DEV)
        s = jnp.where(visible, s, -1e30)
        top = jnp.max(s, axis=0, keepdims=True)
        e = jnp.exp((s - top) * SCALE)
        p = e * (1.0 / jnp.sum(e, axis=0, keepdims=True))
        low = p.astype(BF16)
        o = dot(v, low, (0, 0)).astype(BF16).astype(F32)
        row_dot = jnp.sum(o * do.astype(F32).T, axis=0, keepdims=True)
        gp = dot(v, do, (1, 1))
        gs = (p * (gp - row_dot)).astype(BF16)
        dv = dot(low, do, (1, 0))
        dk = dot(gs, q, (1, 0)) * SCALE
        dq = (dot(k, gs, (0, 0)) * SCALE).T.astype(BF16)
        if b == 0:
            acc[h, 0, pl.ds(0, REACH), :] = dk
            acc[h, 1, pl.ds(0, REACH), :] = dv
            acc[h, 0, pl.ds(REACH, TOK_DEV), :] = jnp.zeros((TOK_DEV, HEAD_WIDTH), F32)
            acc[h, 1, pl.ds(REACH, TOK_DEV), :] = jnp.zeros((TOK_DEV, HEAD_WIDTH), F32)
        else:
            acc[h, 0, key_at, :] += dk
            acc[h, 1, key_at, :] += dv

        @pl.when(core == b)
        def _():
            dq_out[core * MINE + h] = dq

        @pl.when(core != b)
        def _():
            dq_send[h] = dq

    def add_near(h):
        far(h).wait_recv()
        s_out[h] = (acc[h, :, pl.ds(CHIP_TOK, CHIP_TOK), :] + p0_in[h].astype(F32)).astype(BF16)
        near(h).start()

    def finish(h):
        near(h).wait_recv()
        dkv_send[h] = (acc[h, :, other_tok, :] + s_in[h, :, pl.ds(pl.multiple_of(other * TOK_DEV, TOK_DEV), TOK_DEV), :].astype(F32)).astype(BF16)
        give_dkv(h).start()
        dkv_out[core * MINE + h] = (acc[h, :, my_key, :] + s_in[h, :, my_tok, :].astype(F32)).astype(BF16)

    def step(h, carry):
        @pl.when(h + 1 < MINE)
        def _():
            pass_on(h + 1)

        @pl.when(h + 3 < MINE)
        def _():
            send_own(h + 3)

        local_kv(h).wait()
        local_qd(h).wait()
        swap_kv(h).wait_recv()
        swap_qd(h).wait_recv()
        relay(h).wait_recv()
        half(h, 0)
        half(h, 1)
        p0_out[h] = acc[h, :, pl.ds(0, CHIP_TOK), :].astype(BF16)
        far(h).start()
        give_dq(h).start()

        @pl.when(h >= 1)
        def _():
            add_near(h - 1)

        @pl.when(h >= 2)
        def _():
            finish(h - 2)

        return carry

    lax.fori_loop(0, MINE, step, 0)
    finish(MINE - 2)
    add_near(MINE - 1)
    finish(MINE - 1)

    for h in range(MINE):
        take_dq(h).wait_recv()
        take_dkv(h).wait_recv()
        swap_kv(h).wait_send()
        swap_qd(h).wait_send()
        own_same(h).wait_send()
        own_cross(h).wait_send()
        relay(h).wait_send()
        far(h).wait_send()
        near(h).wait_send()
        give_dq(h).wait_send()
        give_dkv(h).wait_send()


def body(n, queries, keys, values, d_out):
    kv = jnp.stack([keys, values]).transpose(2, 0, 1, 3)
    qd = jnp.stack([queries, d_out]).reshape(2, TOK_DEV, KV_HEADS, GROUP, HEAD_WIDTH)
    qd = qd.transpose(2, 0, 1, 3, 4).reshape(KV_HEADS, 2, ROWS, HEAD_WIDTH)
    dma = pltpu.SemaphoreType.DMA
    dq, dkv = pl.pallas_call(
        functools.partial(kernel, n),
        out_shape=(
            jax.ShapeDtypeStruct((KV_HEADS, ROWS, HEAD_WIDTH), BF16),
            jax.ShapeDtypeStruct((KV_HEADS, 2, TOK_DEV, HEAD_WIDTH), BF16),
        ),
        in_specs=[pl.BlockSpec(memory_space=pl.ANY)] * 2,
        out_specs=(pl.BlockSpec(memory_space=pltpu.VMEM), pl.BlockSpec(memory_space=pltpu.VMEM)),
        scratch_shapes=[
            pltpu.VMEM((MINE, 2, SPAN, HEAD_WIDTH), BF16),
            pltpu.VMEM((MINE, 2, 2 * ROWS, HEAD_WIDTH), BF16),
            pltpu.VMEM((MINE, 2, SPAN, HEAD_WIDTH), F32),
            pltpu.VMEM((MINE, 2, CHIP_TOK, HEAD_WIDTH), BF16),
            pltpu.VMEM((MINE, 2, CHIP_TOK, HEAD_WIDTH), BF16),
            pltpu.VMEM((MINE, 2, CHIP_TOK, HEAD_WIDTH), BF16),
            pltpu.VMEM((MINE, 2, CHIP_TOK, HEAD_WIDTH), BF16),
            pltpu.VMEM((MINE, ROWS, HEAD_WIDTH), BF16),
            pltpu.VMEM((MINE, 2, TOK_DEV, HEAD_WIDTH), BF16),
        ]
        + [dma((MINE,))] * 6
        + [dma((MINE, 2))] * 2
        + [dma((MINE,))] * 10,
        compiler_params=pltpu.CompilerParams(collective_id=0, has_side_effects=True, vmem_limit_bytes=48 * 2**20),
    )(kv, qd)
    dq = dq.reshape(KV_HEADS, TOK_DEV, GROUP, HEAD_WIDTH).transpose(1, 0, 2, 3).reshape(TOK_DEV, HEADS, HEAD_WIDTH)
    dkv = dkv.transpose(1, 2, 0, 3)
    return dq, dkv[0], dkv[1]


def solution(mesh):
    placed = P("ctx", None, None)
    return jax.shard_map(
        functools.partial(body, mesh.shape["ctx"]),
        mesh=mesh,
        in_specs=(placed,) * 4,
        out_specs=(placed,) * 3,
        check_vma=False,
    )
```

time: 142 us -> 67.9 us (0.48)
  the two profiles are of different devices: /device:TPU:6 before, /device:TPU:1 now
where the time goes in v1:
time: 67.9 us; the launch traced here: 67.7 us
  Pallas kernels  59.3 us (87%)
  local copies, waits for them, and re-layouts  6.15 us (9%)
  other arithmetic  1.53 us (2%)
  between operations  0.69 us (1%)
    pallas_call x1, Pallas kernels, body(): pl.pallas_call(functools.partial(kernel, n), out_shape=(jax.ShapeDtypeStr...  59.3 us
    unnamed x6, local copies, waits for them, and re-layouts  2.88 us
    another operation x1, other arithmetic, body(): jnp.stack([queries, d_out]).reshape(2, TOK_DEV, KV_HEADS, GROUP, HEAD_WIDTH)  1.48 us

profile of v1, /device:TPU:1, one launch (start us, length us, event | category | flops | bytes accessed | tf_op | source)
XLA Modules:
  0.0 67.7 jit_solution(3239772250204127083)
XLA Ops:
  0.6 1.1 %copy_bitcast_fusion = (bf16[1,128,8,128]{3,1,0,2:T(8,128)(2,1)S(1)}, bf16[1,128,8,128]{3,1,0,2:T(8,128)(2,1)S(1)}) fusion(bf16[128,8,128]{2,1,0:T(8,128)(2,1)} %param.6, bf16[128,8,128]{2,1,0:T(8,128)(2,1)} %param.5), kind=kLoop, calls=%fused_computation.4 | loop fusion | bytes 1048576 | tf_op jit(solution)/shard_map/stack | solution.py:234
  1.8 0.0 copy-start
  1.8 0.0 copy-start.1
  1.8 0.1 maximum_bitcast_fusion.kv_in
  1.8 1.0 %copy-done = bf16[128,16,128]{2,1,0:T(8,128)(2,1)S(1)} copy-done((bf16[128,16,128]{2,1,0:T(8,128)(2,1)S(1)}, bf16[128,16,128]{2,1,0:T(8,128)(2,1)}, u32[]{:S(2)}) %copy-start) | copy-done | bytes 524312
  2.8 0.2 copy-done.1
  3.0 1.5 %pad_maximum_fusion = bf16[2,128,8,2,128]{4,3,2,1,0:T(2,128)(2,1)S(1)} fusion(bf16[1,128,8,2,128]{4,3,2,1,0:T(2,128)(2,1)S(1)} %bitcast.24, bf16[1,128,8,2,128]{4,3,2,1,0:T(2,128)(2,1)S(1)} %bitcast.25), kind=kLoop, calls=%fused_computation | loop fusion | flops 524288 | bytes 2097152 | tf_op jit(solution)/shard_map/stack | solution.py:235
  4.4 1.0 %copy.14 = bf16[2,128,8,2,128]{4,3,1,0,2:T(2,128)(2,1)S(1)} copy(bf16[2,128,8,2,128]{4,3,2,1,0:T(2,128)(2,1)S(1)} %pad_maximum_fusion) | data formatting | bytes 2097152 | tf_op jit(solution)/shard_map/stack | solution.py:235
  5.4 59.3 %shard_map.67 = (bf16[8,256,128]{2,1,0:T(8,128)(2,1)S(1)}, bf16[8,2,128,128]{3,2,1,0:T(8,128)(2,1)S(1)}) custom-call(bf16[8,2,128,128]{3,2,1,0:T(8,128)(2,1)S(1)} %maximum_bitcast_fusion.kv_in, bf16[8,2,256,128]{3,2,1,0:T(8,128)(2,1)S(1)} %bitcast.20), custom_call_target="tpu_custom_call" | custom-call | tf_op jit(solution)/shard_map/pallas_call | solution.py:238
  64.7 1.2 %copy.11 = bf16[128,8,2,128]{3,2,1,0:T(2,128)(2,1)} copy(bf16[128,8,2,128]{3,2,0,1:T(2,128)(2,1)S(1)} %bitcast.22) | data formatting | bytes 1048576 | tf_op jit(solution)/shard_map/transpose | solution.py:262
  65.9 0.9 %copy.13 = bf16[128,8,128]{2,1,0:T(8,128)(2,1)} copy(bf16[128,8,128]{2,0,1:T(8,128)(2,1)S(1)} %get-tuple-element.10) | data formatting | bytes 524288
  66.8 0.9 %copy.12 = bf16[128,8,128]{2,1,0:T(8,128)(2,1)} copy(bf16[128,8,128]{2,0,1:T(8,128)(2,1)S(1)} %get-tuple-element.11) | data formatting | bytes 524288
  (1 shorter events, 0.0 us)
Async XLA Ops:
  1.8 1.0 %copy-start = (bf16[128,16,128]{2,1,0:T(8,128)(2,1)S(1)}, bf16[128,16,128]{2,1,0:T(8,128)(2,1)}, u32[]{:S(2)}) copy-start(bf16[128,16,128]{2,1,0:T(8,128)(2,1)} %param.7) | copy-start | bytes 1572868
  1.8 1.2 %copy-start.1 = (bf16[128,16,128]{2,1,0:T(8,128)(2,1)S(1)}, bf16[128,16,128]{2,1,0:T(8,128)(2,1)}, u32[]{:S(2)}) copy-start(bf16[128,16,128]{2,1,0:T(8,128)(2,1)} %param.4) | copy-start | bytes 1572868

commit v2 on v1

v2 whole, which is shorter than its diff:
```python
import functools

import jax
import jax.numpy as jnp
from jax import lax
from jax.experimental import pallas as pl
from jax.experimental.pallas import tpu as pltpu
from jax.sharding import PartitionSpec as P

HEADS = 16
KV_HEADS = 8
HEAD_WIDTH = 128
WINDOW = 512
TOK_DEV = 128
GROUP = HEADS // KV_HEADS
CHIP_TOK = 2 * TOK_DEV
SPAN = WINDOW + CHIP_TOK
REACH = WINDOW + TOK_DEV
ROWS = GROUP * TOK_DEV
MINE = KV_HEADS // 2

MESH = pl.DeviceIdType.MESH
SCALE = 168.0 ** (-0.5)
F32 = jnp.float32
BF16 = jnp.bfloat16


def dot(a, b, contract):
    return lax.dot_general(a, b, ((contract[:1], contract[1:]), ((), ())), preferred_element_type=F32)


def kernel(
    n, q_in, k_in, v_in, do_in, dq_out, dk_out, dv_out,
    kraw, qraw, kwide, qwide, kv_in, qd_in, dq_wide, dkv_wide,
    kvb, qdb, acc, p0_out, p0_in, s_out, s_in, dq_send, dkv_send, dq_got, dkv_got,
    raw_s, loc_kv, loc_qd, xkv_s, xkv_r, xqd_s, xqd_r, own_s, own_r, fwd_s, fwd_r,
    p0_s, p0_r, sum_s, sum_r, dq_s, dq_r, dkv_s, dkv_r,
):
    me = lax.axis_index("ctx")
    chip = me // 2
    core = me % 2
    other = 1 - core
    partner = chip * 2 + other
    ahead = (me + 2) % n
    ahead_other = (partner + 2) % n
    behind = (me + n - 2) % n
    behind_other = (partner + n - 2) % n
    last = n // 2 - 1
    has_ahead = chip < last
    has_behind = chip > 0
    has_far = chip > 1

    barrier = pltpu.get_barrier_semaphore()

    def greet(*peers):
        for peer in peers:
            pl.semaphore_signal(barrier, inc=1, device_id=(peer,), device_id_type=MESH)

    greet(partner)
    pl.when(has_ahead)(lambda: greet(ahead, ahead_other))
    pl.when(has_behind)(lambda: greet(behind, behind_other))

    raws = [
        pltpu.make_async_copy(src, dst, raw_s.at[i])
        for i, (src, dst) in enumerate(
            ((k_in, kraw.at[0]), (v_in, kraw.at[1]), (q_in, qraw.at[0]), (do_in, qraw.at[1]))
        )
    ]
    for copy in raws:
        copy.start()
    for i in (0, 1):
        raws[i].wait()
        kwide[i] = kraw[i].astype(F32).reshape(TOK_DEV * KV_HEADS, HEAD_WIDTH)
    for g in range(KV_HEADS):
        for i in (0, 1):
            kv_in[g, i] = kwide[i, pl.ds(g, TOK_DEV, KV_HEADS), :].astype(BF16)

    pl.semaphore_wait(barrier, 1 + 2 * has_ahead.astype(jnp.int32) + 2 * has_behind.astype(jnp.int32))

    def remote(src, dst, send, recv, target):
        return pltpu.make_async_remote_copy(
            src_ref=src, dst_ref=dst, send_sem=send, recv_sem=recv, device_id=(target,), device_id_type=MESH
        )

    my_tok = pl.ds(pl.multiple_of(core * TOK_DEV, TOK_DEV), TOK_DEV)
    my_key = pl.ds(pl.multiple_of(WINDOW + core * TOK_DEV, TOK_DEV), TOK_DEV)
    my_back = pl.ds(pl.multiple_of(CHIP_TOK + core * TOK_DEV, TOK_DEV), TOK_DEV)
    my_row = pl.ds(pl.multiple_of(core * ROWS, ROWS), ROWS)
    other_tok = pl.ds(pl.multiple_of(WINDOW + other * TOK_DEV, TOK_DEV), TOK_DEV)
    other_row = pl.ds(pl.multiple_of(other * ROWS, ROWS), ROWS)

    def local_kv(h):
        return pltpu.make_async_copy(kv_in.at[core * MINE + h], kvb.at[h, :, my_key, :], loc_kv.at[h])

    def local_qd(h):
        return pltpu.make_async_copy(qd_in.at[core * MINE + h], qdb.at[h, :, my_row, :], loc_qd.at[h])

    def swap_kv(h):
        return remote(kv_in.at[other * MINE + h], kvb.at[h, :, my_key, :], xkv_s.at[h], xkv_r.at[h], partner)

    def swap_qd(h):
        return remote(qd_in.at[other * MINE + h], qdb.at[h, :, my_row, :], xqd_s.at[h], xqd_r.at[h], partner)

    def own_same(h):
        return remote(kv_in.at[core * MINE + h], kvb.at[h, :, my_back, :], own_s.at[h, 0], own_r.at[h, core], ahead)

    def own_cross(h):
        return remote(kv_in.at[other * MINE + h], kvb.at[h, :, my_back, :], own_s.at[h, 1], own_r.at[h, core], ahead_other)

    def came(h, j):
        tok = pl.ds(pl.multiple_of(CHIP_TOK + j * TOK_DEV, TOK_DEV), TOK_DEV)
        return remote(kvb.at[h, :, tok, :], kvb.at[h, :, tok, :], own_s.at[h, j], own_r.at[h, j], ahead)

    def relay(h, j):
        tok = pl.ds(pl.multiple_of(CHIP_TOK + j * TOK_DEV, TOK_DEV), TOK_DEV)
        to = pl.ds(pl.multiple_of(j * TOK_DEV, TOK_DEV), TOK_DEV)
        return remote(kvb.at[h, :, tok, :], kvb.at[h, :, to, :], fwd_s.at[h, j], fwd_r.at[h, j], ahead)

    def far(h, a):
        return remote(p0_out.at[h, a], p0_in.at[h, a], p0_s.at[h, a], p0_r.at[h, a], behind)

    def near(h, a):
        return remote(s_out.at[h, a], s_in.at[h, a], sum_s.at[h, a], sum_r.at[h, a], behind)

    def give_dq(h):
        return remote(dq_send.at[h], dq_got.at[h], dq_s.at[h], dq_r.at[h], partner)

    def give_dkv(h):
        return remote(dkv_send.at[h], dkv_got.at[h], dkv_s.at[h], dkv_r.at[h], partner)

    def send_own(h):
        @pl.when(has_ahead)
        def _():
            own_same(h).start()
            own_cross(h).start()

    def pass_on(h, j):
        @pl.when(has_behind)
        def _():
            came(h, j).wait_recv()

        @pl.when(has_behind & has_ahead)
        def _():
            relay(h, j).start()

    send_own(0)
    for h in range(MINE):
        local_kv(h).start()
        swap_kv(h).start()
    for i in (0, 1):
        raws[2 + i].wait()
        qwide[i] = qraw[i].astype(F32).reshape(TOK_DEV * HEADS, HEAD_WIDTH)
    for g in range(KV_HEADS):
        for i in (0, 1):
            for r in range(GROUP):
                qd_in[g, i, pl.ds(r * TOK_DEV, TOK_DEV), :] = qwide[i, pl.ds(g * GROUP + r, TOK_DEV, HEADS), :].astype(BF16)
    for h in range(MINE):
        local_qd(h).start()
        swap_qd(h).start()

    @pl.when(chip == 0)
    def _():
        kvb[:, :, pl.ds(0, WINDOW), :] = jnp.zeros((MINE, 2, WINDOW, HEAD_WIDTH), BF16)

    @pl.when(chip == 1)
    def _():
        kvb[:, :, pl.ds(0, CHIP_TOK), :] = jnp.zeros((MINE, 2, CHIP_TOK, HEAD_WIDTH), BF16)

    pass_on(0, core)
    pass_on(0, other)
    send_own(1)
    send_own(2)

    first_key = WINDOW - CHIP_TOK * chip

    def keep_dq(g, rows):
        for r in range(GROUP):
            dq_wide[pl.ds(g * GROUP + r, TOK_DEV, HEADS), :] = rows[r * TOK_DEV : (r + 1) * TOK_DEV]

    def keep_dkv(g, pair):
        for i in (0, 1):
            dkv_wide[i, pl.ds(g, TOK_DEV, KV_HEADS), :] = pair[i]

    def half(h, b):
        key_at = pl.ds(b * TOK_DEV, REACH)
        row_at = pl.ds(b * ROWS, ROWS)
        k = kvb[h, 0, key_at, :]
        v = kvb[h, 1, key_at, :]
        q = qdb[h, 0, row_at, :]
        do = qdb[h, 1, row_at, :]
        s = dot(k, q, (1, 1))
        key_pos = lax.broadcasted_iota(jnp.int32, (REACH, ROWS), 0)
        query_pos = lax.broadcasted_iota(jnp.int32, (REACH, ROWS), 1) % TOK_DEV
        distance = key_pos - query_pos
        visible = (distance > 0) & (distance <= WINDOW) & (key_pos >= first_key - b * TOK_DEV)
        s = jnp.where(visible, s, -1e30)
        top = jnp.max(s, axis=0, keepdims=True)
        e = jnp.exp((s - top) * SCALE)
        p = e * (1.0 / jnp.sum(e, axis=0, keepdims=True))
        low = p.astype(BF16)
        o = dot(v, low, (0, 0)).astype(BF16).astype(F32)
        row_dot = jnp.sum(o * do.astype(F32).T, axis=0, keepdims=True)
        gp = dot(v, do, (1, 1))
        gs = (p * (gp - row_dot)).astype(BF16)
        dv = dot(low, do, (1, 0))
        dk = dot(gs, q, (1, 0)) * SCALE
        dq = (dot(k, gs, (0, 0)) * SCALE).T
        if b == 0:
            acc[h, 0, pl.ds(0, REACH), :] = dk
            acc[h, 1, pl.ds(0, REACH), :] = dv
            acc[h, 0, pl.ds(REACH, TOK_DEV), :] = jnp.zeros((TOK_DEV, HEAD_WIDTH), F32)
            acc[h, 1, pl.ds(REACH, TOK_DEV), :] = jnp.zeros((TOK_DEV, HEAD_WIDTH), F32)
        else:
            acc[h, 0, key_at, :] += dk
            acc[h, 1, key_at, :] += dv

        @pl.when(core == b)
        def _():
            keep_dq(core * MINE + h, dq)

        @pl.when(core != b)
        def _():
            dq_send[h] = dq.astype(BF16)

    def send_far(h, a):
        @pl.when(has_far)
        def _():
            p0_out[h, a] = acc[h, :, pl.ds(a * TOK_DEV, TOK_DEV), :].astype(BF16)
            far(h, a).start()

    def add_near(h, a):
        at = pl.ds(CHIP_TOK + a * TOK_DEV, TOK_DEV)

        @pl.when(has_behind & has_ahead)
        def _():
            far(h, a).wait_recv()
            s_out[h, a] = (acc[h, :, at, :] + p0_in[h, a].astype(F32)).astype(BF16)

        @pl.when(chip == last)
        def _():
            s_out[h, a] = acc[h, :, at, :].astype(BF16)

        @pl.when(has_behind)
        def _():
            near(h, a).start()

    def finish(h, a):
        at = pl.ds(WINDOW + a * TOK_DEV, TOK_DEV)

        @pl.when(has_ahead)
        def _():
            near(h, a).wait_recv()

        @pl.when(chip == last)
        def _():
            s_in[h, a] = jnp.zeros((2, TOK_DEV, HEAD_WIDTH), BF16)

        total = acc[h, :, at, :] + s_in[h, a].astype(F32)

        @pl.when(core == a)
        def _():
            keep_dkv(core * MINE + h, total)

        @pl.when(core != a)
        def _():
            dkv_send[h] = total.astype(BF16)
            give_dkv(h).start()

    def pass_both(h):
        pass_on(h, core)
        pass_on(h, other)

    def add_both(h):
        add_near(h, 0)
        add_near(h, 1)

    def finish_both(h):
        finish(h, 0)
        finish(h, 1)

    def step(h, carry):
        local_kv(h).wait()
        local_qd(h).wait()
        swap_kv(h).wait_recv()
        swap_qd(h).wait_recv()

        @pl.when(has_far)
        def _():
            relay(h, 0).wait_recv()
            relay(h, 1).wait_recv()

        half(h, 0)
        send_far(h, 0)

        @pl.when(h == 0)
        def _():
            pass_on(1, core)

        half(h, 1)
        send_far(h, 1)
        give_dq(h).start()

        @pl.when(h == 0)
        def _():
            pass_on(1, other)
            send_own(3)

        @pl.when(h + 2 < MINE)
        def _():
            pass_both(h + 2)
            add_both(h)

        @pl.when(h == MINE - 1)
        def _():
            add_both(h - 1)

        @pl.when((h >= 1) & (h + 1 < MINE))
        def _():
            finish_both(h - 1)

        return carry

    lax.fori_loop(0, MINE, step, 0)
    add_both(MINE - 1)
    finish_both(MINE - 2)
    finish_both(MINE - 1)

    for h in range(MINE):
        give_dq(h).wait_recv()
        keep_dq(other * MINE + h, dq_got[h].astype(F32))
    dq_out[...] = dq_wide[...].astype(BF16).reshape(TOK_DEV, HEADS, HEAD_WIDTH)
    for h in range(MINE):
        give_dkv(h).wait_recv()
        keep_dkv(other * MINE + h, dkv_got[h].astype(F32))
    dk_out[...] = dkv_wide[0].astype(BF16).reshape(TOK_DEV, KV_HEADS, HEAD_WIDTH)
    dv_out[...] = dkv_wide[1].astype(BF16).reshape(TOK_DEV, KV_HEADS, HEAD_WIDTH)

    for h in range(MINE):
        swap_kv(h).wait_send()
        swap_qd(h).wait_send()
        give_dq(h).wait_send()
        give_dkv(h).wait_send()

    @pl.when(has_ahead)
    def _():
        for h in range(MINE):
            own_same(h).wait_send()
            own_cross(h).wait_send()

    @pl.when(has_behind & has_ahead)
    def _():
        for h in range(MINE):
            relay(h, 0).wait_send()
            relay(h, 1).wait_send()

    @pl.when(has_far)
    def _():
        for h in range(MINE):
            far(h, 0).wait_send()
            far(h, 1).wait_send()

    @pl.when(has_behind)
    def _():
        for h in range(MINE):
            near(h, 0).wait_send()
            near(h, 1).wait_send()


def body(n, queries, keys, values, d_out):
    dma = pltpu.SemaphoreType.DMA
    wide = (TOK_DEV, HEADS, HEAD_WIDTH)
    slim = (TOK_DEV, KV_HEADS, HEAD_WIDTH)
    return pl.pallas_call(
        functools.partial(kernel, n),
        out_shape=(
            jax.ShapeDtypeStruct(wide, BF16),
            jax.ShapeDtypeStruct(slim, BF16),
            jax.ShapeDtypeStruct(slim, BF16),
        ),
        in_specs=[pl.BlockSpec(memory_space=pltpu.HBM)] * 4,
        out_specs=(pl.BlockSpec(memory_space=pltpu.VMEM),) * 3,
        scratch_shapes=[
            pltpu.VMEM((2,) + slim, BF16),
            pltpu.VMEM((2,) + wide, BF16),
            pltpu.VMEM((2, TOK_DEV * KV_HEADS, HEAD_WIDTH), F32),
            pltpu.VMEM((2, TOK_DEV * HEADS, HEAD_WIDTH), F32),
            pltpu.VMEM((KV_HEADS, 2, TOK_DEV, HEAD_WIDTH), BF16),
            pltpu.VMEM((KV_HEADS, 2, ROWS, HEAD_WIDTH), BF16),
            pltpu.VMEM((TOK_DEV * HEADS, HEAD_WIDTH), F32),
            pltpu.VMEM((2, TOK_DEV * KV_HEADS, HEAD_WIDTH), F32),
            pltpu.VMEM((MINE, 2, SPAN, HEAD_WIDTH), BF16),
            pltpu.VMEM((MINE, 2, 2 * ROWS, HEAD_WIDTH), BF16),
            pltpu.VMEM((MINE, 2, SPAN, HEAD_WIDTH), F32),
            pltpu.VMEM((MINE, 2, 2, TOK_DEV, HEAD_WIDTH), BF16),
            pltpu.VMEM((MINE, 2, 2, TOK_DEV, HEAD_WIDTH), BF16),
            pltpu.VMEM((MINE, 2, 2, TOK_DEV, HEAD_WIDTH), BF16),
            pltpu.VMEM((MINE, 2, 2, TOK_DEV, HEAD_WIDTH), BF16),
            pltpu.VMEM((MINE, ROWS, HEAD_WIDTH), BF16),
            pltpu.VMEM((MINE, 2, TOK_DEV, HEAD_WIDTH), BF16),
            pltpu.VMEM((MINE, ROWS, HEAD_WIDTH), BF16),
            pltpu.VMEM((MINE, 2, TOK_DEV, HEAD_WIDTH), BF16),
            dma((4,)),
        ]
        + [dma((MINE,))] * 6
        + [dma((MINE, 2))] * 8
        + [dma((MINE,))] * 4,
        compiler_params=pltpu.CompilerParams(collective_id=0, has_side_effects=True, vmem_limit_bytes=60 * 1024 * 1024),
    )(queries, keys, values, d_out)


def solution(mesh):
    placed = P("ctx", None, None)
    return jax.shard_map(
        functools.partial(body, mesh.shape["ctx"]),
        mesh=mesh,
        in_specs=(placed,) * 4,
        out_specs=(placed,) * 3,
        check_vma=False,
    )
```

time: 67.9 us -> 58.9 us (0.87)
  the two profiles are of different devices: /device:TPU:1 before, /device:TPU:6 now
where the time goes in v2:
time: 58.9 us; the launch traced here: 58 us
  Pallas kernels  53.7 us (91%)
  local copies, waits for them, and re-layouts  3.66 us (6%)
  between operations  0.65 us (1%)
    pallas_call x1, Pallas kernels, body(): pl.pallas_call(functools.partial(kernel, n), out_shape=(jax.ShapeDtypeStr...  53.7 us
    unnamed x7, local copies, waits for them, and re-layouts  3.66 us

profile of v2, /device:TPU:6, one launch (start us, length us, event | category | flops | bytes accessed | tf_op | source)
XLA Modules:
  0.0 58.0 jit_solution(15901766862310013611)
XLA Ops:
  0.6 53.7 %shard_map.67 = (bf16[128,16,128]{2,1,0:T(8,128)(2,1)}, bf16[128,8,128]{2,1,0:T(8,128)(2,1)}, bf16[128,8,128]{2,1,0:T(8,128)(2,1)}) custom-call(bf16[128,16,128]{2,1,0:T(8,128)(2,1)} %q_in.1, bf16[128,8,128]{2,1,0:T(8,128)(2,1)} %k_in.1, bf16[128,8,128]{2,1,0:T(8,128)(2,1)} %v_in.1, bf16[128,16,128]{2,1,0:T(8,128)(2,1)} %do_in.1), custom_call_target="tpu_custom_call" | custom-call | tf_op jit(solution)/shard_map/pallas_call | solution.py:373
  54.3 0.0 copy-start.1
  54.3 1.9 %copy.10 = bf16[128,16,128]{2,1,0:T(8,128)(2,1)} copy(bf16[128,16,128]{2,1,0:T(8,128)(2,1)} %get-tuple-element.6) | data formatting | bytes 1048576
  56.3 0.0 copy-done.1
  56.3 0.0 copy-start
  56.3 0.7 %copy.11 = bf16[128,8,128]{2,1,0:T(8,128)(2,1)} copy(bf16[128,8,128]{2,1,0:T(8,128)(2,1)S(1)} %copy-done.1) | data formatting | bytes 524288
  57.0 0.3 copy-done
  57.3 0.7 %copy.12 = bf16[128,8,128]{2,1,0:T(8,128)(2,1)} copy(bf16[128,8,128]{2,1,0:T(8,128)(2,1)S(1)} %copy-done) | data formatting | bytes 524288
Async XLA Ops:
  54.3 1.9 %copy-start.1 = (bf16[128,8,128]{2,1,0:T(8,128)(2,1)S(1)}, bf16[128,8,128]{2,1,0:T(8,128)(2,1)}, u32[]{:S(2)}) copy-start(bf16[128,8,128]{2,1,0:T(8,128)(2,1)} %get-tuple-element.7) | copy-start | bytes 786436
  56.3 1.0 %copy-start = (bf16[128,8,128]{2,1,0:T(8,128)(2,1)S(1)}, bf16[128,8,128]{2,1,0:T(8,128)(2,1)}, u32[]{:S(2)}) copy-start(bf16[128,8,128]{2,1,0:T(8,128)(2,1)} %get-tuple-element.8) | copy-start | bytes 786436

commit v3 on v2

--- a/solution.py
+++ b/solution.py
@@ -32,7 +32,7 @@
 def kernel(
     n, q_in, k_in, v_in, do_in, dq_out, dk_out, dv_out,
     kraw, qraw, kwide, qwide, kv_in, qd_in, dq_wide, dkv_wide,
-    kvb, qdb, acc, p0_out, p0_in, s_out, s_in, dq_send, dkv_send, dq_got, dkv_got,
+    kvb, qdb, acc, p0_out, p0_in, s_out, s_in, dq_send, dq_got, dkv_got,
     raw_s, loc_kv, loc_qd, xkv_s, xkv_r, xqd_s, xqd_r, own_s, own_r, fwd_s, fwd_r,
     p0_s, p0_r, sum_s, sum_r, dq_s, dq_r, dkv_s, dkv_r,
 ):
@@ -57,7 +57,6 @@
             pl.semaphore_signal(barrier, inc=1, device_id=(peer,), device_id_type=MESH)
 
     greet(partner)
-    pl.when(has_ahead)(lambda: greet(ahead, ahead_other))
     pl.when(has_behind)(lambda: greet(behind, behind_other))
 
     raws = [
@@ -75,7 +74,7 @@
         for i in (0, 1):
             kv_in[g, i] = kwide[i, pl.ds(g, TOK_DEV, KV_HEADS), :].astype(BF16)
 
-    pl.semaphore_wait(barrier, 1 + 2 * has_ahead.astype(jnp.int32) + 2 * has_behind.astype(jnp.int32))
+    pl.semaphore_wait(barrier, 1 + 2 * has_ahead.astype(jnp.int32))
 
     def remote(src, dst, send, recv, target):
         return pltpu.make_async_remote_copy(
@@ -120,13 +119,17 @@
         return remote(p0_out.at[h, a], p0_in.at[h, a], p0_s.at[h, a], p0_r.at[h, a], behind)
 
     def near(h, a):
-        return remote(s_out.at[h, a], s_in.at[h, a], sum_s.at[h, a], sum_r.at[h, a], behind)
+        g = core * MINE + h
+        return remote(s_out.at[h, a], s_in.at[g], sum_s.at[h, a], sum_r.at[g], behind - core + a)
+
+    def near_in(g):
+        return remote(s_in.at[g], s_in.at[g], sum_s.at[0, 0], sum_r.at[g], behind)
 
     def give_dq(h):
         return remote(dq_send.at[h], dq_got.at[h], dq_s.at[h], dq_r.at[h], partner)
 
     def give_dkv(h):
-        return remote(dkv_send.at[h], dkv_got.at[h], dkv_s.at[h], dkv_r.at[h], partner)
+        return remote(acc.at[h, :, other_tok, :], dkv_got.at[h], dkv_s.at[h], dkv_r.at[h], partner)
 
     def send_own(h):
         @pl.when(has_ahead)
@@ -143,7 +146,17 @@
         def _():
             relay(h, j).start()
 
+    def pass_both(h):
+        pass_on(h, core)
+        pass_on(h, other)
+
     send_own(0)
+
+    @pl.when(chip == 1)
+    def _():
+        for h in range(1, MINE):
+            send_own(h)
+
     for h in range(MINE):
         local_kv(h).start()
         swap_kv(h).start()
@@ -166,20 +179,29 @@
     def _():
         kvb[:, :, pl.ds(0, CHIP_TOK), :] = jnp.zeros((MINE, 2, CHIP_TOK, HEAD_WIDTH), BF16)
 
-    pass_on(0, core)
-    pass_on(0, other)
-    send_own(1)
-    send_own(2)
+    pass_both(0)
+
+    @pl.when(chip != 1)
+    def _():
+        send_own(1)
+        send_own(2)
+
+    pass_both(1)
+
+    @pl.when(chip != 1)
+    def _():
+        send_own(3)
+
+    @pl.when(chip == 2)
+    def _():
+        pass_both(2)
+        pass_both(3)
 
     first_key = WINDOW - CHIP_TOK * chip
 
     def keep_dq(g, rows):
         for r in range(GROUP):
             dq_wide[pl.ds(g * GROUP + r, TOK_DEV, HEADS), :] = rows[r * TOK_DEV : (r + 1) * TOK_DEV]
-
-    def keep_dkv(g, pair):
-        for i in (0, 1):
-            dkv_wide[i, pl.ds(g, TOK_DEV, KV_HEADS), :] = pair[i]
 
     def half(h, b):
         key_at = pl.ds(b * TOK_DEV, REACH)
@@ -244,39 +266,29 @@
         def _():
             near(h, a).start()
 
-    def finish(h, a):
-        at = pl.ds(WINDOW + a * TOK_DEV, TOK_DEV)
-
+    def finish(g, own):
         @pl.when(has_ahead)
         def _():
-            near(h, a).wait_recv()
+            near_in(g).wait_recv()
 
         @pl.when(chip == last)
         def _():
-            s_in[h, a] = jnp.zeros((2, TOK_DEV, HEAD_WIDTH), BF16)
-
-        total = acc[h, :, at, :] + s_in[h, a].astype(F32)
-
-        @pl.when(core == a)
-        def _():
-            keep_dkv(core * MINE + h, total)
-
-        @pl.when(core != a)
-        def _():
-            dkv_send[h] = total.astype(BF16)
-            give_dkv(h).start()
-
-    def pass_both(h):
-        pass_on(h, core)
-        pass_on(h, other)
+            s_in[g] = jnp.zeros((2, TOK_DEV, HEAD_WIDTH), BF16)
+
+        total = own + s_in[g].astype(F32)
+        for i in (0, 1):
+            dkv_wide[i, pl.ds(g, TOK_DEV, KV_HEADS), :] = total[i]
+
+    def finish_both(h):
+        give_dq(h).wait_recv()
+        keep_dq(other * MINE + h, dq_got[h].astype(F32))
+        give_dkv(h).wait_recv()
+        finish(core * MINE + h, acc[h, :, my_key, :])
+        finish(other * MINE + h, dkv_got[h])
 
     def add_both(h):
         add_near(h, 0)
         add_near(h, 1)
-
-    def finish_both(h):
-        finish(h, 0)
-        finish(h, 1)
 
     def step(h, carry):
         local_kv(h).wait()
@@ -292,22 +304,17 @@
         half(h, 0)
         send_far(h, 0)
 
-        @pl.when(h == 0)
-        def _():
-            pass_on(1, core)
-
         half(h, 1)
         send_far(h, 1)
         give_dq(h).start()
-
-        @pl.when(h == 0)
-        def _():
-            pass_on(1, other)
-            send_own(3)
+        give_dkv(h).start()
+
+        @pl.when((h + 2 < MINE) & (chip != 2))
+        def _():
+            pass_both(h + 2)
 
         @pl.when(h + 2 < MINE)
         def _():
-            pass_both(h + 2)
             add_both(h)
 
         @pl.when(h == MINE - 1)
@@ -323,15 +330,12 @@
     lax.fori_loop(0, MINE, step, 0)
     add_both(MINE - 1)
     finish_both(MINE - 2)
-    finish_both(MINE - 1)
-
-    for h in range(MINE):
-        give_dq(h).wait_recv()
-        keep_dq(other * MINE + h, dq_got[h].astype(F32))
+    give_dq(MINE - 1).wait_recv()
+    keep_dq(other * MINE + MINE - 1, dq_got[MINE - 1].astype(F32))
     dq_out[...] = dq_wide[...].astype(BF16).reshape(TOK_DEV, HEADS, HEAD_WIDTH)
-    for h in range(MINE):
-        give_dkv(h).wait_recv()
-        keep_dkv(other * MINE + h, dkv_got[h].astype(F32))
+    give_dkv(MINE - 1).wait_recv()
+    finish(core * MINE + MINE - 1, acc[MINE - 1, :, my_key, :])
+    finish(other * MINE + MINE - 1, dkv_got[MINE - 1])
     dk_out[...] = dkv_wide[0].astype(BF16).reshape(TOK_DEV, KV_HEADS, HEAD_WIDTH)
     dv_out[...] = dkv_wide[1].astype(BF16).reshape(TOK_DEV, KV_HEADS, HEAD_WIDTH)
 
@@ -394,18 +398,18 @@
             pltpu.VMEM((MINE, 2, 2, TOK_DEV, HEAD_WIDTH), BF16),
             pltpu.VMEM((MINE, 2, 2, TOK_DEV, HEAD_WIDTH), BF16),
             pltpu.VMEM((MINE, 2, 2, TOK_DEV, HEAD_WIDTH), BF16),
-            pltpu.VMEM((MINE, 2, 2, TOK_DEV, HEAD_WIDTH), BF16),
+            pltpu.VMEM((KV_HEADS, 2, TOK_DEV, HEAD_WIDTH), BF16),
             pltpu.VMEM((MINE, ROWS, HEAD_WIDTH), BF16),
-            pltpu.VMEM((MINE, 2, TOK_DEV, HEAD_WIDTH), BF16),
             pltpu.VMEM((MINE, ROWS, HEAD_WIDTH), BF16),
-            pltpu.VMEM((MINE, 2, TOK_DEV, HEAD_WIDTH), BF16),
+            pltpu.VMEM((MINE, 2, TOK_DEV, HEAD_WIDTH), F32),
             dma((4,)),
         ]
         + [dma((MINE,))] * 6
-        + [dma((MINE, 2))] * 8
+        + [dma((MINE, 2))] * 7
+        + [dma((KV_HEADS,))]
         + [dma((MINE,))] * 4,
-        compiler_params=pltpu.CompilerParams(collective_id=0, has_side_effects=True, vmem_limit_bytes=60 * 1024 * 1024),
-    )(queries, keys, values, d_out)
+        compiler_params=pltpu.CompilerParams(collective_id=0, has_side_effects=True, vmem_limit_bytes=48000 * 1024),
+    )(*(pltpu.with_memory_space_constraint(a, pltpu.HBM) for a in (queries, keys, values, d_out)))
 
 
 def solution(mesh):

time: 58.9 us -> 55.8 us (0.947); the launches traced: 58 us -> 55.6 us
  local copies, waits for them, and re-layouts: 3.66 us -> 2.2 us
  Pallas kernels: 53.7 us -> 52.8 us
    unnamed x7 -> x3, local copies, waits for them, and re-layouts: 3.66 us -> 2.2 us
    pallas_call x1, Pallas kernels: 53.7 us -> 52.8 us  [body(): pl.pallas_call(functools.partial(kernel, n), out_shape=(jax.ShapeDtypeStr...]
where the time goes in v3:
time: 55.8 us; the launch traced here: 55.6 us
  Pallas kernels  52.8 us (95%)
  local copies, waits for them, and re-layouts  2.2 us (4%)
  between operations  0.64 us (1%)
    pallas_call x1, Pallas kernels, body(): pl.pallas_call(functools.partial(kernel, n), out_shape=(jax.ShapeDtypeStr...  52.8 us
    unnamed x3, local copies, waits for them, and re-layouts  2.2 us

profile of v3, /device:TPU:6, one launch (start us, length us, event | category | flops | bytes accessed | tf_op | source)
XLA Modules:
  0.0 55.6 jit_solution(16647951706250187730)
XLA Ops:
  0.6 52.8 %shard_map.67 = (bf16[128,16,128]{2,1,0:T(8,128)(2,1)S(1)}, bf16[128,8,128]{2,1,0:T(8,128)(2,1)S(1)}, bf16[128,8,128]{2,1,0:T(8,128)(2,1)S(1)}) custom-call(bf16[128,16,128]{2,1,0:T(8,128)(2,1)} %q_in.1, bf16[128,8,128]{2,1,0:T(8,128)(2,1)} %k_in.1, bf16[128,8,128]{2,1,0:T(8,128)(2,1)} %v_in.1, bf16[128,16,128]{2,1,0:T(8,128)(2,1)} %do_in.1), custom_call_target="tpu_custom_call" | custom-call | tf_op jit(solution)/shard_map/pallas_call | solution.py:377
  53.4 0.8 %copy.10 = bf16[128,16,128]{2,1,0:T(8,128)(2,1)} copy(bf16[128,16,128]{2,1,0:T(8,128)(2,1)S(1)} %get-tuple-element.6) | data formatting | bytes 1048576
  54.2 0.7 %copy.11 = bf16[128,8,128]{2,1,0:T(8,128)(2,1)} copy(bf16[128,8,128]{2,1,0:T(8,128)(2,1)S(1)} %get-tuple-element.7) | data formatting | bytes 524288
  54.9 0.7 %copy.12 = bf16[128,8,128]{2,1,0:T(8,128)(2,1)} copy(bf16[128,8,128]{2,1,0:T(8,128)(2,1)S(1)} %get-tuple-element.8) | data formatting | bytes 524288

commit v4 on v3

--- a/solution.py
+++ b/solution.py
@@ -18,6 +18,9 @@
 REACH = WINDOW + TOK_DEV
 ROWS = GROUP * TOK_DEV
 MINE = KV_HEADS // 2
+ROUND = 1
+LAST = MINE - 1
+RING = 4
 
 MESH = pl.DeviceIdType.MESH
 SCALE = 168.0 ** (-0.5)
@@ -32,9 +35,10 @@
 def kernel(
     n, q_in, k_in, v_in, do_in, dq_out, dk_out, dv_out,
     kraw, qraw, kwide, qwide, kv_in, qd_in, dq_wide, dkv_wide,
-    kvb, qdb, acc, p0_out, p0_in, s_out, s_in, dq_send, dq_got, dkv_got,
+    kvb, qdb, acc, p0_out, p0_in, s_out, s_in, dq_send, dq_got, dkv_got, rb, cb, pc_in,
     raw_s, loc_kv, loc_qd, xkv_s, xkv_r, xqd_s, xqd_r, own_s, own_r, fwd_s, fwd_r,
     p0_s, p0_r, sum_s, sum_r, dq_s, dq_r, dkv_s, dkv_r,
+    b1_s, b1_r, b2_s, c1_s, c1_r, c2_s, c2_r,
 ):
     me = lax.axis_index("ctx")
     chip = me // 2
@@ -49,6 +53,18 @@
     has_ahead = chip < last
     has_behind = chip > 0
     has_far = chip > 1
+    row = chip // RING * RING
+    up = row + (chip + 1) % RING
+    down = row + (chip + RING - 1) % RING
+    has_two = chip + 2 <= last
+    up_two = up + 2 <= last
+    down_two = down >= 2
+
+    def ring_of(c, d):
+        return c // RING * RING + (c + d) % RING
+
+    def dev(c, k):
+        return c * 2 + k
 
     barrier = pltpu.get_barrier_semaphore()
 
@@ -57,7 +73,10 @@
             pl.semaphore_signal(barrier, inc=1, device_id=(peer,), device_id_type=MESH)
 
     greet(partner)
+    greet(dev(up, 0), dev(up, 1), dev(down, core))
     pl.when(has_behind)(lambda: greet(behind, behind_other))
+    pl.when(has_far)(lambda: greet(dev(ring_of(chip - 2, RING - 1), core)))
+    pl.when(has_two)(lambda: greet(dev(ring_of(chip + 2, 1), 0), dev(ring_of(chip + 2, 1), 1)))
 
     raws = [
         pltpu.make_async_copy(src, dst, raw_s.at[i])
@@ -74,7 +93,8 @@
         for i in (0, 1):
             kv_in[g, i] = kwide[i, pl.ds(g, TOK_DEV, KV_HEADS), :].astype(BF16)
 
-    pl.semaphore_wait(barrier, 1 + 2 * has_ahead.astype(jnp.int32))
+    known = 2 * has_ahead.astype(jnp.int32) + up_two.astype(jnp.int32) + 2 * down_two.astype(jnp.int32)
+    pl.semaphore_wait(barrier, 4 + known)
 
     def remote(src, dst, send, recv, target):
         return pltpu.make_async_remote_copy(
@@ -131,6 +151,29 @@
     def give_dkv(h):
         return remote(acc.at[h, :, other_tok, :], dkv_got.at[h], dkv_s.at[h], dkv_r.at[h], partner)
 
+    def round_same():
+        return remote(kv_in.at[core * MINE + ROUND], rb.at[:, my_tok, :], b1_s.at[0], b1_r.at[core], dev(down, core))
+
+    def round_cross():
+        return remote(kv_in.at[other * MINE + ROUND], rb.at[:, my_tok, :], b1_s.at[1], b1_r.at[core], dev(down, other))
+
+    def round_on(j):
+        tok = pl.ds(pl.multiple_of(j * TOK_DEV, TOK_DEV), TOK_DEV)
+        return remote(rb.at[:, tok, :], kvb.at[ROUND, :, tok, :], b2_s.at[j], fwd_r.at[ROUND, j], dev(up + 2, core))
+
+    def round_came(j):
+        tok = pl.ds(pl.multiple_of(j * TOK_DEV, TOK_DEV), TOK_DEV)
+        return remote(rb.at[:, tok, :], rb.at[:, tok, :], b2_s.at[j], b1_r.at[j], ahead)
+
+    def back(a):
+        return remote(p0_out.at[LAST, a], cb.at[a], c1_s.at[a], c1_r.at[a], dev(up, core))
+
+    def back_on(a):
+        return remote(cb.at[a], pc_in.at[core], c2_s.at[a], c2_r.at[core], dev(down - 2, a))
+
+    def back_came(k):
+        return remote(pc_in.at[k], pc_in.at[k], c2_s.at[0], c2_r.at[k], ahead)
+
     def send_own(h):
         @pl.when(has_ahead)
         def _():
@@ -151,6 +194,11 @@
         pass_on(h, other)
 
     send_own(0)
+
+    @pl.when(has_two)
+    def _():
+        round_same().start()
+        round_cross().start()
 
     @pl.when(chip == 1)
     def _():
@@ -183,14 +231,14 @@
 
     @pl.when(chip != 1)
     def _():
-        send_own(1)
-        send_own(2)
-
-    pass_both(1)
-
-    @pl.when(chip != 1)
-    def _():
-        send_own(3)
+        for h in range(1, MINE):
+            send_own(h)
+
+    @pl.when(up_two)
+    def _():
+        for j in (core, other):
+            round_came(j).wait_recv()
+            round_on(j).start()
 
     @pl.when(chip == 2)
     def _():
@@ -248,17 +296,24 @@
         @pl.when(has_far)
         def _():
             p0_out[h, a] = acc[h, :, pl.ds(a * TOK_DEV, TOK_DEV), :].astype(BF16)
+
+        @pl.when(has_far & (h < LAST))
+        def _():
             far(h, a).start()
+
+        @pl.when(has_far & (h == LAST))
+        def _():
+            back(a).start()
 
     def add_near(h, a):
         at = pl.ds(CHIP_TOK + a * TOK_DEV, TOK_DEV)
 
-        @pl.when(has_behind & has_ahead)
+        @pl.when(has_behind & has_ahead & (h < LAST))
         def _():
             far(h, a).wait_recv()
             s_out[h, a] = (acc[h, :, at, :] + p0_in[h, a].astype(F32)).astype(BF16)
 
-        @pl.when(chip == last)
+        @pl.when((chip == last) | (h == LAST))
         def _():
             s_out[h, a] = acc[h, :, at, :].astype(BF16)
 
@@ -280,8 +335,6 @@
             dkv_wide[i, pl.ds(g, TOK_DEV, KV_HEADS), :] = total[i]
 
     def finish_both(h):
-        give_dq(h).wait_recv()
-        keep_dq(other * MINE + h, dq_got[h].astype(F32))
         give_dkv(h).wait_recv()
         finish(core * MINE + h, acc[h, :, my_key, :])
         finish(other * MINE + h, dkv_got[h])
@@ -301,6 +354,11 @@
             relay(h, 0).wait_recv()
             relay(h, 1).wait_recv()
 
+        @pl.when(has_behind & (h == ROUND))
+        def _():
+            came(ROUND, 0).wait_recv()
+            came(ROUND, 1).wait_recv()
+
         half(h, 0)
         send_far(h, 0)
 
@@ -309,33 +367,57 @@
         give_dq(h).start()
         give_dkv(h).start()
 
-        @pl.when((h + 2 < MINE) & (chip != 2))
-        def _():
-            pass_both(h + 2)
-
-        @pl.when(h + 2 < MINE)
-        def _():
-            add_both(h)
-
-        @pl.when(h == MINE - 1)
-        def _():
-            add_both(h - 1)
-
-        @pl.when((h >= 1) & (h + 1 < MINE))
-        def _():
-            finish_both(h - 1)
+        @pl.when((h == 1) & (chip != 2))
+        def _():
+            pass_both(2)
+
+        @pl.when(h == 1)
+        def _():
+            add_both(0)
+
+        @pl.when((h == 1) & (chip != 2))
+        def _():
+            pass_both(3)
+
+        @pl.when(h == 1)
+        def _():
+            add_both(1)
+
+        @pl.when(h == 2)
+        def _():
+            finish_both(0)
 
         return carry
 
     lax.fori_loop(0, MINE, step, 0)
-    add_both(MINE - 1)
-    finish_both(MINE - 2)
-    give_dq(MINE - 1).wait_recv()
-    keep_dq(other * MINE + MINE - 1, dq_got[MINE - 1].astype(F32))
+    add_both(LAST)
+    add_both(2)
+
+    @pl.when(down_two)
+    def _():
+        for a in (0, 1):
+            back(a).wait_recv()
+            back_on(a).start()
+
+    finish_both(1)
+    for h in range(MINE):
+        give_dq(h).wait_recv()
+        keep_dq(other * MINE + h, dq_got[h].astype(F32))
     dq_out[...] = dq_wide[...].astype(BF16).reshape(TOK_DEV, HEADS, HEAD_WIDTH)
-    give_dkv(MINE - 1).wait_recv()
-    finish(core * MINE + MINE - 1, acc[MINE - 1, :, my_key, :])
-    finish(other * MINE + MINE - 1, dkv_got[MINE - 1])
+    finish_both(2)
+    give_dkv(LAST).wait_recv()
+
+    @pl.when(has_two)
+    def _():
+        back_came(0).wait_recv()
+        back_came(1).wait_recv()
+
+    @pl.when(chip + 2 > last)
+    def _():
+        pc_in[...] = jnp.zeros_like(pc_in)
+
+    finish(core * MINE + LAST, acc[LAST, :, my_key, :] + pc_in[core].astype(F32))
+    finish(other * MINE + LAST, dkv_got[LAST] + pc_in[other].astype(F32))
     dk_out[...] = dkv_wide[0].astype(BF16).reshape(TOK_DEV, KV_HEADS, HEAD_WIDTH)
     dv_out[...] = dkv_wide[1].astype(BF16).reshape(TOK_DEV, KV_HEADS, HEAD_WIDTH)
 
@@ -353,15 +435,32 @@
 
     @pl.when(has_behind & has_ahead)
     def _():
-        for h in range(MINE):
+        for h in (0, 2, 3):
             relay(h, 0).wait_send()
             relay(h, 1).wait_send()
 
+    @pl.when(has_two)
+    def _():
+        round_same().wait_send()
+        round_cross().wait_send()
+
+    @pl.when(up_two)
+    def _():
+        round_on(0).wait_send()
+        round_on(1).wait_send()
+
     @pl.when(has_far)
     def _():
-        for h in range(MINE):
+        for h in range(LAST):
             far(h, 0).wait_send()
             far(h, 1).wait_send()
+        back(0).wait_send()
+        back(1).wait_send()
+
+    @pl.when(down_two)
+    def _():
+        back_on(0).wait_send()
+        back_on(1).wait_send()
 
     @pl.when(has_behind)
     def _():
@@ -402,12 +501,16 @@
             pltpu.VMEM((MINE, ROWS, HEAD_WIDTH), BF16),
             pltpu.VMEM((MINE, ROWS, HEAD_WIDTH), BF16),
             pltpu.VMEM((MINE, 2, TOK_DEV, HEAD_WIDTH), F32),
+            pltpu.VMEM((2, CHIP_TOK, HEAD_WIDTH), BF16),
+            pltpu.VMEM((2, 2, TOK_DEV, HEAD_WIDTH), BF16),
+            pltpu.VMEM((2, 2, TOK_DEV, HEAD_WIDTH), BF16),
             dma((4,)),
         ]
         + [dma((MINE,))] * 6
         + [dma((MINE, 2))] * 7
         + [dma((KV_HEADS,))]
-        + [dma((MINE,))] * 4,
+        + [dma((MINE,))] * 4
+        + [dma((2,))] * 7,
         compiler_params=pltpu.CompilerParams(collective_id=0, has_side_effects=True, vmem_limit_bytes=48000 * 1024),
     )(*(pltpu.with_memory_space_constraint(a, pltpu.HBM) for a in (queries, keys, values, d_out)))
 

time: 55.8 us -> 54 us (0.968)
  the two profiles are of different devices: /device:TPU:6 before, /device:TPU:49 now
where the time goes in v4:
time: 54 us; the launch traced here: 53.8 us
  Pallas kernels  51 us (94%)
  local copies, waits for them, and re-layouts  2.2 us (4%)
  between operations  0.64 us (1%)
    pallas_call x1, Pallas kernels, body(): pl.pallas_call(functools.partial(kernel, n), out_shape=(jax.ShapeDtypeStr...  51 us
    unnamed x3, local copies, waits for them, and re-layouts  2.2 us

profile of v4, /device:TPU:49, one launch (start us, length us, event | category | flops | bytes accessed | tf_op | source)
XLA Modules:
  0.0 53.8 jit_solution(232536689686380002)
XLA Ops:
  0.6 51.0 %shard_map.67 = (bf16[128,16,128]{2,1,0:T(8,128)(2,1)S(1)}, bf16[128,8,128]{2,1,0:T(8,128)(2,1)S(1)}, bf16[128,8,128]{2,1,0:T(8,128)(2,1)S(1)}) custom-call(bf16[128,16,128]{2,1,0:T(8,128)(2,1)} %q_in.1, bf16[128,8,128]{2,1,0:T(8,128)(2,1)} %k_in.1, bf16[128,8,128]{2,1,0:T(8,128)(2,1)} %v_in.1, bf16[128,16,128]{2,1,0:T(8,128)(2,1)} %do_in.1), custom_call_target="tpu_custom_call" | custom-call | tf_op jit(solution)/shard_map/pallas_call | solution.py:476
  51.6 0.8 %copy.10 = bf16[128,16,128]{2,1,0:T(8,128)(2,1)} copy(bf16[128,16,128]{2,1,0:T(8,128)(2,1)S(1)} %get-tuple-element.6) | data formatting | bytes 1048576
  52.4 0.7 %copy.11 = bf16[128,8,128]{2,1,0:T(8,128)(2,1)} copy(bf16[128,8,128]{2,1,0:T(8,128)(2,1)S(1)} %get-tuple-element.7) | data formatting | bytes 524288
  53.1 0.7 %copy.12 = bf16[128,8,128]{2,1,0:T(8,128)(2,1)} copy(bf16[128,8,128]{2,1,0:T(8,128)(2,1)S(1)} %get-tuple-element.8) | data formatting | bytes 524288

commit v5 on v4

--- a/solution.py
+++ b/solution.py
@@ -24,6 +24,7 @@
 
 MESH = pl.DeviceIdType.MESH
 SCALE = 168.0 ** (-0.5)
+HIDDEN = -1e30
 F32 = jnp.float32
 BF16 = jnp.bfloat16
 
@@ -75,6 +76,10 @@
     greet(partner)
     greet(dev(up, 0), dev(up, 1), dev(down, core))
     pl.when(has_behind)(lambda: greet(behind, behind_other))
+    depth = chip // RING % 16
+    early = chip < n // 8
+    for d in (1, 2):
+        pl.when(early & (depth >= d))(lambda d=d: greet(dev(chip - RING * d, core)))
     pl.when(has_far)(lambda: greet(dev(ring_of(chip - 2, RING - 1), core)))
     pl.when(has_two)(lambda: greet(dev(ring_of(chip + 2, 1), 0), dev(ring_of(chip + 2, 1), 1)))
 
@@ -94,6 +99,8 @@
             kv_in[g, i] = kwide[i, pl.ds(g, TOK_DEV, KV_HEADS), :].astype(BF16)
 
     known = 2 * has_ahead.astype(jnp.int32) + up_two.astype(jnp.int32) + 2 * down_two.astype(jnp.int32)
+    for d in (1, 2):
+        known = known + (early & (depth + d < 16)).astype(jnp.int32)
     pl.semaphore_wait(barrier, 4 + known)
 
     def remote(src, dst, send, recv, target):
@@ -259,11 +266,15 @@
         q = qdb[h, 0, row_at, :]
         do = qdb[h, 1, row_at, :]
         s = dot(k, q, (1, 1))
-        key_pos = lax.broadcasted_iota(jnp.int32, (REACH, ROWS), 0)
-        query_pos = lax.broadcasted_iota(jnp.int32, (REACH, ROWS), 1) % TOK_DEV
-        distance = key_pos - query_pos
-        visible = (distance > 0) & (distance <= WINDOW) & (key_pos >= first_key - b * TOK_DEV)
-        s = jnp.where(visible, s, -1e30)
+        key_at_tile = lax.broadcasted_iota(jnp.int32, (TOK_DEV, ROWS), 0)
+        query_at_tile = lax.broadcasted_iota(jnp.int32, (TOK_DEV, ROWS), 1) % TOK_DEV
+        later = key_at_tile > query_at_tile
+        tiles = [s[i * TOK_DEV : (i + 1) * TOK_DEV] for i in range(REACH // TOK_DEV)]
+        tiles[0] = jnp.where(later, tiles[0], HIDDEN)
+        tiles[-1] = jnp.where(later, HIDDEN, tiles[-1])
+        for i in range(WINDOW // TOK_DEV - b):
+            tiles[i] = tiles[i] + jnp.where((b + i) * TOK_DEV >= first_key, 0.0, HIDDEN)
+        s = jnp.concatenate(tiles, axis=0)
         top = jnp.max(s, axis=0, keepdims=True)
         e = jnp.exp((s - top) * SCALE)
         p = e * (1.0 / jnp.sum(e, axis=0, keepdims=True))
@@ -469,11 +480,19 @@
             near(h, 1).wait_send()
 
 
+def put(*refs):
+    copies = [pltpu.make_async_copy(refs[i], refs[3 + i], refs[6].at[i]) for i in range(3)]
+    for copy in copies:
+        copy.start()
+    for copy in copies:
+        copy.wait()
+
+
 def body(n, queries, keys, values, d_out):
     dma = pltpu.SemaphoreType.DMA
     wide = (TOK_DEV, HEADS, HEAD_WIDTH)
     slim = (TOK_DEV, KV_HEADS, HEAD_WIDTH)
-    return pl.pallas_call(
+    grads = pl.pallas_call(
         functools.partial(kernel, n),
         out_shape=(
             jax.ShapeDtypeStruct(wide, BF16),
@@ -513,6 +532,14 @@
         + [dma((2,))] * 7,
         compiler_params=pltpu.CompilerParams(collective_id=0, has_side_effects=True, vmem_limit_bytes=48000 * 1024),
     )(*(pltpu.with_memory_space_constraint(a, pltpu.HBM) for a in (queries, keys, values, d_out)))
+    return pl.pallas_call(
+        put,
+        out_shape=tuple(jax.ShapeDtypeStruct(g.shape, g.dtype) for g in grads),
+        in_specs=[pl.BlockSpec(memory_space=pltpu.VMEM)] * 3,
+        out_specs=(pl.BlockSpec(memory_space=pltpu.HBM),) * 3,
+        scratch_shapes=[dma((3,))],
+        compiler_params=pltpu.CompilerParams(vmem_limit_bytes=32 * 2**20),
+    )(*grads)
 
 
 def solution(mesh):

time: 54 us -> 49.3 us (0.913)
  the two profiles are of different devices: /device:TPU:49 before, /device:TPU:1 now
where the time goes in v5:
time: 49.3 us; the launch traced here: 49.2 us
  Pallas kernels  48.5 us (98%)
  between operations  0.64 us (1%)
    pallas_call x1, Pallas kernels, body(): pl.pallas_call(functools.partial(kernel, n), out_shape=(jax.ShapeDtypeStr...  47.5 us
    pallas_call x1, Pallas kernels, body(): pl.pallas_call(put, out_shape=tuple((jax.ShapeDtypeStruct(g.shape, g.dtyp...  0.99 us

profile of v5, /device:TPU:1, one launch (start us, length us, event | category | flops | bytes accessed | tf_op | source)
XLA Modules:
  0.0 49.2 jit_solution(2964629319510066970)
XLA Ops:
  0.6 47.5 %shard_map.67 = (bf16[128,16,128]{2,1,0:T(8,128)(2,1)S(1)}, bf16[128,8,128]{2,1,0:T(8,128)(2,1)S(1)}, bf16[128,8,128]{2,1,0:T(8,128)(2,1)S(1)}) custom-call(bf16[128,16,128]{2,1,0:T(8,128)(2,1)} %q_in.1, bf16[128,8,128]{2,1,0:T(8,128)(2,1)} %k_in.1, bf16[128,8,128]{2,1,0:T(8,128)(2,1)} %v_in.1, bf16[128,16,128]{2,1,0:T(8,128)(2,1)} %do_in.1), custom_call_target="tpu_custom_call" | custom-call | tf_op jit(solution)/shard_map/pallas_call | solution.py:495
  48.2 1.0 %shard_map.68 = (bf16[128,16,128]{2,1,0:T(8,128)(2,1)}, bf16[128,8,128]{2,1,0:T(8,128)(2,1)}, bf16[128,8,128]{2,1,0:T(8,128)(2,1)}) custom-call(bf16[128,16,128]{2,1,0:T(8,128)(2,1)S(1)} %get-tuple-element.6.refs_0_, bf16[128,8,128]{2,1,0:T(8,128)(2,1)S(1)} %get-tuple-element.7.refs_1_, bf16[128,8,128]{2,1,0:T(8,128)(2,1)S(1)} %get-tuple-element.8.refs_2_), custom_call_target="tpu_custom_call" | custom-call | tf_op jit(solution)/shard_map/pallas_call | solution.py:535
